TPU v7x, 128 devices: a whole 4x4x4 slice. The times are simulated.
128 devices in a mesh: wide: 16 (over x, z), narrow: 8 (over y, core).
Axes of the slice: x: 4, y: 4, z: 4, core: 2. Of those that a mesh axis runs over, the one named last changes fastest.
Arguments:
- tensor_slab: float32 [512, 512, 2048], P(None, 'wide', 'narrow'), may hold values from -220 to 220
- start_basis: float32 [512, 64], replicated, may hold values from -6 to 6
Outputs:
- factor_basis: float32 [512, 64], replicated
- core_unfold: float32 [2048, 64, 512], P('narrow', 'wide')
All inputs are finite; a program needn't handle non-finite values.
Results may differ from a plain program's by a relative error of at most 0.0003.
Values sent between devices are 32-bit elements; how exact they have to be, the bound alone decides.
A program may use at most 64 MiB of HBM per device.

v0:
```python
import jax
import jax.numpy as jnp
from jax import lax
from jax.sharding import PartitionSpec as P

I1 = 512
ITERS = 8


def orthonormal(block, inner):
    lower_factor = jnp.linalg.cholesky(inner)
    return jax.scipy.linalg.solve_triangular(lower_factor, block.T, lower=True).T


def shards(tensor_slab, start_basis):
    highest = lax.Precision.HIGHEST
    unfold = tensor_slab.reshape(I1, -1)
    basis = start_basis
    local_gram = jnp.dot(unfold, unfold.T, precision=highest, preferred_element_type=jnp.float32)
    gram_full = lax.psum(local_gram, ("wide", "narrow"))
    for sweep_index in range(ITERS):
        block = jnp.dot(gram_full, basis, precision=highest)
        basis = orthonormal(block, jnp.dot(block.T, block, precision=highest))
    core_local = jnp.einsum("ir,ijl->lrj", basis, tensor_slab, precision=highest)
    core_unfold = lax.all_to_all(core_local, "wide", split_axis=1, concat_axis=2, tiled=True)
    return (basis, core_unfold)


def solution(mesh):
    placed = (P(None, "wide", "narrow"), P())
    return jax.shard_map(
        shards,
        mesh=mesh,
        in_specs=placed,
        out_specs=(P(), P("narrow", "wide", None)),
        check_vma=False,
    )
```

profile of v0, /device:TPU:1, one launch (start us, length us, event | category | flops | bytes accessed | tf_op | source)
XLA Modules:
  0.0 389.1 jit_solution(11629814040123961032)
XLA Ops:
  7.2 40.1 %fusion.7 = f32[512,512]{1,0:T(8,128)} fusion(f32[512,32,256]{2,1,0:T(8,128)} %param.5), kind=kOutput, calls=%fused_computation.5 | convolution fusion | flops 25769803776 | bytes 17825792 | tf_op jit(solution)/shard_map/dot_general | solution.py:19
  47.3 150.7 %all-reduce.2.cloned.1.call-done = f32[512,512]{1,0:T(8,128)} async-done(((f32[512,512]{1,0:T(8,128)}), f32[512,512]{1,0:T(8,128)}) %all-reduce.2.cloned.1.call-update) | async-done | bytes 1048592 | tf_op jit(solution)/shard_map/psum | solution.py:20
  198.0 2.4 fusion.65
  200.7 5.8 %cholesky.134 = f32[64,64]{1,0:T(8,128)S(1)} custom-call(f32[64,64]{1,0:T(8,128)S(1)} %fusion.50), custom_call_target="Cholesky" | custom-call | tf_op jit(solution)/shard_map/jit(cholesky)/cholesky | solution.py:11
  206.6 0.6 compare_reduce_fusion.7
  207.3 0.7 fusion.27
  207.9 4.9 %custom-call.12 = f32[1,64,64]{1,2,0:T(8,128)S(1)} custom-call(f32[1,64,64]{2,1,0:T(8,128)S(1)} %fusion.27), custom_call_target="InvertDiagBlocksLowerTriangular" | custom-call | tf_op jit(solution)/shard_map/jit(_solve_triangular)/triangular_solve | solution.py:12
  213.2 2.4 fusion.67
  215.9 5.8 %cholesky.145 = f32[64,64]{1,0:T(8,128)S(1)} custom-call(f32[64,64]{1,0:T(8,128)S(1)} %fusion.48), custom_call_target="Cholesky" | custom-call | tf_op jit(solution)/shard_map/jit(cholesky)/cholesky | solution.py:11
  221.8 0.6 compare_reduce_fusion.6
  222.4 0.7 fusion.28
  223.1 4.9 %custom-call.13 = f32[1,64,64]{1,2,0:T(8,128)S(1)} custom-call(f32[1,64,64]{2,1,0:T(8,128)S(1)} %fusion.28), custom_call_target="InvertDiagBlocksLowerTriangular" | custom-call | tf_op jit(solution)/shard_map/jit(_solve_triangular)/triangular_solve | solution.py:12
  228.3 2.4 fusion.69
  231.0 5.8 %cholesky.156 = f32[64,64]{1,0:T(8,128)S(1)} custom-call(f32[64,64]{1,0:T(8,128)S(1)} %fusion.46), custom_call_target="Cholesky" | custom-call | tf_op jit(solution)/shard_map/jit(cholesky)/cholesky | solution.py:11
  236.9 0.6 compare_reduce_fusion.5
  237.6 0.7 fusion.29
  238.2 4.9 %custom-call.14 = f32[1,64,64]{1,2,0:T(8,128)S(1)} custom-call(f32[1,64,64]{2,1,0:T(8,128)S(1)} %fusion.29), custom_call_target="InvertDiagBlocksLowerTriangular" | custom-call | tf_op jit(solution)/shard_map/jit(_solve_triangular)/triangular_solve | solution.py:12
  243.1 0.3 fusion.21
  243.5 2.4 fusion.71
  246.2 5.8 %cholesky.167 = f32[64,64]{1,0:T(8,128)S(1)} custom-call(f32[64,64]{1,0:T(8,128)S(1)} %fusion.44), custom_call_target="Cholesky" | custom-call | tf_op jit(solution)/shard_map/jit(cholesky)/cholesky | solution.py:11
  252.1 0.6 compare_reduce_fusion.4
  252.7 0.7 fusion.30
  253.4 4.9 %custom-call.15 = f32[1,64,64]{1,2,0:T(8,128)S(1)} custom-call(f32[1,64,64]{2,1,0:T(8,128)S(1)} %fusion.30), custom_call_target="InvertDiagBlocksLowerTriangular" | custom-call | tf_op jit(solution)/shard_map/jit(_solve_triangular)/triangular_solve | solution.py:12
  258.3 0.3 fusion.19
  258.6 2.5 fusion.73
  261.5 5.8 %cholesky.178 = f32[64,64]{1,0:T(8,128)S(1)} custom-call(f32[64,64]{1,0:T(8,128)S(1)} %fusion.42), custom_call_target="Cholesky" | custom-call | tf_op jit(solution)/shard_map/jit(cholesky)/cholesky | solution.py:11
  267.4 0.6 compare_reduce_fusion.3
  268.0 0.7 fusion.31
  268.7 4.9 %custom-call.16 = f32[1,64,64]{1,2,0:T(8,128)S(1)} custom-call(f32[1,64,64]{2,1,0:T(8,128)S(1)} %fusion.31), custom_call_target="InvertDiagBlocksLowerTriangular" | custom-call | tf_op jit(solution)/shard_map/jit(_solve_triangular)/triangular_solve | solution.py:12
  273.9 2.4 fusion.75
  276.6 5.8 %cholesky.189 = f32[64,64]{1,0:T(8,128)S(1)} custom-call(f32[64,64]{1,0:T(8,128)S(1)} %fusion.40), custom_call_target="Cholesky" | custom-call | tf_op jit(solution)/shard_map/jit(cholesky)/cholesky | solution.py:11
  282.5 0.6 compare_reduce_fusion.2
  283.2 0.7 fusion.32
  283.8 4.9 %custom-call.17 = f32[1,64,64]{1,2,0:T(8,128)S(1)} custom-call(f32[1,64,64]{2,1,0:T(8,128)S(1)} %fusion.32), custom_call_target="InvertDiagBlocksLowerTriangular" | custom-call | tf_op jit(solution)/shard_map/jit(_solve_triangular)/triangular_solve | solution.py:12
  289.1 2.4 fusion.77
  291.8 5.8 %cholesky.200 = f32[64,64]{1,0:T(8,128)S(1)} custom-call(f32[64,64]{1,0:T(8,128)S(1)} %fusion.38), custom_call_target="Cholesky" | custom-call | tf_op jit(solution)/shard_map/jit(cholesky)/cholesky | solution.py:11
  297.7 0.6 compare_reduce_fusion.1
  298.3 0.7 fusion.33
  299.0 4.9 %custom-call.18 = f32[1,64,64]{1,2,0:T(8,128)S(1)} custom-call(f32[1,64,64]{2,1,0:T(8,128)S(1)} %fusion.33), custom_call_target="InvertDiagBlocksLowerTriangular" | custom-call | tf_op jit(solution)/shard_map/jit(_solve_triangular)/triangular_solve | solution.py:12
  304.2 2.4 fusion.79
  306.9 5.8 %cholesky.211 = f32[64,64]{1,0:T(8,128)S(1)} custom-call(f32[64,64]{1,0:T(8,128)S(1)} %fusion.36), custom_call_target="Cholesky" | custom-call | tf_op jit(solution)/shard_map/jit(cholesky)/cholesky | solution.py:11
  312.8 0.6 compare_reduce_fusion
  313.5 0.7 fusion.34
  314.1 4.9 %custom-call.19 = f32[1,64,64]{1,2,0:T(8,128)S(1)} custom-call(f32[1,64,64]{2,1,0:T(8,128)S(1)} %fusion.34), custom_call_target="InvertDiagBlocksLowerTriangular" | custom-call | tf_op jit(solution)/shard_map/jit(_solve_triangular)/triangular_solve | solution.py:12
  319.4 25.8 %fusion.4 = f32[256,64,32]{0,1,2:T(8,128)S(1)} fusion(f32[512,32,256]{2,1,0:T(8,128)} %param.5, f32[64,512]{1,0:T(8,128)S(1)} %fusion.11), kind=kOutput, calls=%fused_computation.4 | convolution fusion | flops 3221225472 | bytes 19005440 | tf_op jit(solution)/shard_map/ir,ijl->lrj/dot_general | solution.py:24
  345.2 1.2 copy.53
  346.4 33.5 %all_to_all.18 = f32[256,64,32]{0,2,1:T(8,128)S(1)} all-to-all(f32[256,64,32]{0,2,1:T(8,128)S(1)} %copy.53), channel_id=1, replica_groups=mesh['wide'=16,'narrow'=8] {'wide'}, dimensions={1} | all-to-all | bytes 4194304 | tf_op jit(solution)/shard_map/all_to_all | solution.py:25
  380.1 2.0 copy.55
  (45 shorter events, 5.2 us)
Async XLA Ops:
  7.2 190.9 %copy-start = (f32[512,64]{0,1:T(8,128)S(1)}, f32[512,64]{0,1:T(8,128)}, u32[]{:S(2)}) copy-start(f32[512,64]{0,1:T(8,128)} %param.6) | copy-start | bytes 393220
  7.2 190.9 %all-reduce.2.cloned.1.call-start = ((), (), s32[]{:S(2)}) async-start(), calls=%async_computation.1 | async-start | bytes 2097152 | tf_op jit(solution)/shard_map/psum | solution.py:20
  319.4 62.7 %copy-start.1 = (f32[64,512]{1,0:T(8,128)}, f32[64,512]{1,0:T(8,128)S(1)}, u32[]{:S(2)}) copy-start(f32[64,512]{1,0:T(8,128)S(1)} %fusion.11) | copy-start | bytes 393220
Sparse Core Ops, SparseCore 0:
  47.4 150.5 all-reduce.1
where the time goes:
time: 393 us; the launch traced here: 389 us
  waiting for transfers between devices  151 us (38%)
  other arithmetic  96.6 us (25%)
  matrix products  89.7 us (23%)
  blocking collectives  33.5 us (9%)
  between operations  14.6 us (4%)
  local copies, waits for them, and re-layouts  3.93 us (1%)
    psum x1, waiting for transfers between devices, shards(): gram_full = lax.psum(local_gram, ('wide', 'narrow'))  151 us
    another operation x24, other arithmetic, orthonormal(): lower_factor = jnp.linalg.cholesky(inner)  52.2 us
    another operation x16, other arithmetic, orthonormal(): jax.scipy.linalg.solve_triangular(lower_factor, block.T, lower=True)  44.4 us
    dot_general x1, matrix products, shards(): jnp.dot(unfold, unfold.T, precision=highest, preferred_element_type=jnp.f...  40.1 us
    all_to_all x1, blocking collectives, shards(): lax.all_to_all(core_local, 'wide', split_axis=1, concat_axis=2, tiled=True)  33.5 us
    dot_general x1, matrix products, shards(): jnp.einsum('ir,ijl->lrj', basis, tensor_slab, precision=highest)  25.8 us
    dot_general x8, matrix products, shards(): block = jnp.dot(gram_full, basis, precision=highest)  19 us
  transfers between devices with their start and end apart: 1, of which 1 were waited for; matrix products, arithmetic and copies ran while one was open for 0% of the time, Pallas kernels for 0%

commit v1 on v0

--- a/solution.py
+++ b/solution.py
@@ -17,7 +17,7 @@
     unfold = tensor_slab.reshape(I1, -1)
     basis = start_basis
     local_gram = jnp.dot(unfold, unfold.T, precision=highest, preferred_element_type=jnp.float32)
-    gram_full = lax.psum(local_gram, ("wide", "narrow"))
+    gram_full = lax.psum(lax.psum(local_gram, "wide"), "narrow")
     for sweep_index in range(ITERS):
         block = jnp.dot(gram_full, basis, precision=highest)
         basis = orthonormal(block, jnp.dot(block.T, block, precision=highest))

time: 393 us -> 396 us (level)
  the two profiles are of different devices: /device:TPU:1 before, /device:TPU:24 now
where the time goes in v1:
time: 396 us; the launch traced here: 392 us
  waiting for transfers between devices  151 us (38%)
  other arithmetic  96.6 us (24%)
  matrix products  89.3 us (23%)
  blocking collectives  36.3 us (9%)
  between operations  14.6 us (4%)
    psum x2, waiting for transfers between devices, shards(): gram_full = lax.psum(lax.psum(local_gram, 'wide'), 'narrow')  151 us
    another operation x24, other arithmetic, orthonormal(): lower_factor = jnp.linalg.cholesky(inner)  52.2 us
    another operation x16, other arithmetic, orthonormal(): jax.scipy.linalg.solve_triangular(lower_factor, block.T, lower=True)  44.4 us
    dot_general x1, matrix products, shards(): jnp.dot(unfold, unfold.T, precision=highest, preferred_element_type=jnp.f...  39.6 us
    all_to_all x1, blocking collectives, shards(): lax.all_to_all(core_local, 'wide', split_axis=1, concat_axis=2, tiled=True)  36.3 us
    dot_general x1, matrix products, shards(): jnp.einsum('ir,ijl->lrj', basis, tensor_slab, precision=highest)  25.8 us
    dot_general x8, matrix products, shards(): block = jnp.dot(gram_full, basis, precision=highest)  19 us
  transfers between devices with their start and end apart: 2, of which 2 were waited for; matrix products, arithmetic and copies ran while one was open for 0% of the time, Pallas kernels for 0%

profile of v1, /device:TPU:24, one launch (start us, length us, event | category | flops | bytes accessed | tf_op | source)
XLA Modules:
  0.0 391.8 jit_solution(14627306743008608503)
XLA Ops:
  7.2 39.6 %fusion.7 = f32[512,512]{1,0:T(8,128)} fusion(f32[512,32,256]{2,1,0:T(8,128)} %param.5), kind=kOutput, calls=%fused_computation.5 | convolution fusion | flops 25769803776 | bytes 17825792 | tf_op jit(solution)/shard_map/dot_general | solution.py:19
  46.9 0.5 all-reduce.5.cloned.1.call-start
  47.4 89.0 %all-reduce.3.cloned.1.call-done = f32[512,512]{1,0:T(8,128)} async-done(((f32[512,512]{1,0:T(8,128)}), f32[512,512]{1,0:T(8,128)}) %all-reduce.3.cloned.1.call-update) | async-done | bytes 1048592 | tf_op jit(solution)/shard_map/psum | solution.py:20
  136.4 61.6 %all-reduce.5.cloned.1.call-done = f32[512,512]{1,0:T(8,128)} async-done(((f32[512,512]{1,0:T(8,128)}), f32[512,512]{1,0:T(8,128)}) %all-reduce.5.cloned.1.call-update) | async-done | bytes 1048592 | tf_op jit(solution)/shard_map/psum | solution.py:20
  197.9 2.4 fusion.65
  200.7 5.8 %cholesky.134 = f32[64,64]{1,0:T(8,128)S(1)} custom-call(f32[64,64]{1,0:T(8,128)S(1)} %fusion.50), custom_call_target="Cholesky" | custom-call | tf_op jit(solution)/shard_map/jit(cholesky)/cholesky | solution.py:11
  206.5 0.6 compare_reduce_fusion.7
  207.2 0.7 fusion.27
  207.8 4.9 %custom-call.12 = f32[1,64,64]{1,2,0:T(8,128)S(1)} custom-call(f32[1,64,64]{2,1,0:T(8,128)S(1)} %fusion.27), custom_call_target="InvertDiagBlocksLowerTriangular" | custom-call | tf_op jit(solution)/shard_map/jit(_solve_triangular)/triangular_solve | solution.py:12
  213.1 2.4 fusion.67
  215.8 5.8 %cholesky.145 = f32[64,64]{1,0:T(8,128)S(1)} custom-call(f32[64,64]{1,0:T(8,128)S(1)} %fusion.48), custom_call_target="Cholesky" | custom-call | tf_op jit(solution)/shard_map/jit(cholesky)/cholesky | solution.py:11
  221.7 0.6 compare_reduce_fusion.6
  222.3 0.7 fusion.28
  223.0 4.9 %custom-call.13 = f32[1,64,64]{1,2,0:T(8,128)S(1)} custom-call(f32[1,64,64]{2,1,0:T(8,128)S(1)} %fusion.28), custom_call_target="InvertDiagBlocksLowerTriangular" | custom-call | tf_op jit(solution)/shard_map/jit(_solve_triangular)/triangular_solve | solution.py:12
  228.2 2.4 fusion.69
  231.0 5.8 %cholesky.156 = f32[64,64]{1,0:T(8,128)S(1)} custom-call(f32[64,64]{1,0:T(8,128)S(1)} %fusion.46), custom_call_target="Cholesky" | custom-call | tf_op jit(solution)/shard_map/jit(cholesky)/cholesky | solution.py:11
  236.8 0.6 compare_reduce_fusion.5
  237.5 0.7 fusion.29
  238.1 4.9 %custom-call.14 = f32[1,64,64]{1,2,0:T(8,128)S(1)} custom-call(f32[1,64,64]{2,1,0:T(8,128)S(1)} %fusion.29), custom_call_target="InvertDiagBlocksLowerTriangular" | custom-call | tf_op jit(solution)/shard_map/jit(_solve_triangular)/triangular_solve | solution.py:12
  243.4 2.4 fusion.71
  246.1 5.8 %cholesky.167 = f32[64,64]{1,0:T(8,128)S(1)} custom-call(f32[64,64]{1,0:T(8,128)S(1)} %fusion.44), custom_call_target="Cholesky" | custom-call | tf_op jit(solution)/shard_map/jit(cholesky)/cholesky | solution.py:11
  252.0 0.6 compare_reduce_fusion.4
  252.6 0.7 fusion.30
  253.3 4.9 %custom-call.15 = f32[1,64,64]{1,2,0:T(8,128)S(1)} custom-call(f32[1,64,64]{2,1,0:T(8,128)S(1)} %fusion.30), custom_call_target="InvertDiagBlocksLowerTriangular" | custom-call | tf_op jit(solution)/shard_map/jit(_solve_triangular)/triangular_solve | solution.py:12
  258.5 2.5 fusion.73
  261.4 5.8 %cholesky.178 = f32[64,64]{1,0:T(8,128)S(1)} custom-call(f32[64,64]{1,0:T(8,128)S(1)} %fusion.42), custom_call_target="Cholesky" | custom-call | tf_op jit(solution)/shard_map/jit(cholesky)/cholesky | solution.py:11
  267.3 0.6 compare_reduce_fusion.3
  268.0 0.7 fusion.31
  268.6 4.9 %custom-call.16 = f32[1,64,64]{1,2,0:T(8,128)S(1)} custom-call(f32[1,64,64]{2,1,0:T(8,128)S(1)} %fusion.31), custom_call_target="InvertDiagBlocksLowerTriangular" | custom-call | tf_op jit(solution)/shard_map/jit(_solve_triangular)/triangular_solve | solution.py:12
  273.9 2.4 fusion.75
  276.6 5.8 %cholesky.189 = f32[64,64]{1,0:T(8,128)S(1)} custom-call(f32[64,64]{1,0:T(8,128)S(1)} %fusion.40), custom_call_target="Cholesky" | custom-call | tf_op jit(solution)/shard_map/jit(cholesky)/cholesky | solution.py:11
  282.5 0.6 compare_reduce_fusion.2
  283.1 0.7 fusion.32
  283.8 4.9 %custom-call.17 = f32[1,64,64]{1,2,0:T(8,128)S(1)} custom-call(f32[1,64,64]{2,1,0:T(8,128)S(1)} %fusion.32), custom_call_target="InvertDiagBlocksLowerTriangular" | custom-call | tf_op jit(solution)/shard_map/jit(_solve_triangular)/triangular_solve | solution.py:12
  289.0 2.4 fusion.77
  291.7 5.8 %cholesky.200 = f32[64,64]{1,0:T(8,128)S(1)} custom-call(f32[64,64]{1,0:T(8,128)S(1)} %fusion.38), custom_call_target="Cholesky" | custom-call | tf_op jit(solution)/shard_map/jit(cholesky)/cholesky | solution.py:11
  297.6 0.6 compare_reduce_fusion.1
  298.2 0.7 fusion.33
  298.9 4.9 %custom-call.18 = f32[1,64,64]{1,2,0:T(8,128)S(1)} custom-call(f32[1,64,64]{2,1,0:T(8,128)S(1)} %fusion.33), custom_call_target="InvertDiagBlocksLowerTriangular" | custom-call | tf_op jit(solution)/shard_map/jit(_solve_triangular)/triangular_solve | solution.py:12
  304.1 2.4 fusion.79
  306.9 5.8 %cholesky.211 = f32[64,64]{1,0:T(8,128)S(1)} custom-call(f32[64,64]{1,0:T(8,128)S(1)} %fusion.36), custom_call_target="Cholesky" | custom-call | tf_op jit(solution)/shard_map/jit(cholesky)/cholesky | solution.py:11
  312.7 0.6 compare_reduce_fusion
  313.4 0.7 fusion.34
  314.0 4.9 %custom-call.19 = f32[1,64,64]{1,2,0:T(8,128)S(1)} custom-call(f32[1,64,64]{2,1,0:T(8,128)S(1)} %fusion.34), custom_call_target="InvertDiagBlocksLowerTriangular" | custom-call | tf_op jit(solution)/shard_map/jit(_solve_triangular)/triangular_solve | solution.py:12
  319.3 25.8 %fusion.4 = f32[256,64,32]{0,1,2:T(8,128)S(1)} fusion(f32[512,32,256]{2,1,0:T(8,128)} %param.5, f32[64,512]{1,0:T(8,128)S(1)} %fusion.11), kind=kOutput, calls=%fused_computation.4 | convolution fusion | flops 3221225472 | bytes 19005440 | tf_op jit(solution)/shard_map/ir,ijl->lrj/dot_general | solution.py:24
  345.1 1.2 copy.53
  346.4 36.3 %all_to_all.18 = f32[256,64,32]{0,2,1:T(8,128)S(1)} all-to-all(f32[256,64,32]{0,2,1:T(8,128)S(1)} %copy.53), channel_id=1, replica_groups=mesh['wide'=16,'narrow'=8] {'wide'}, dimensions={1} | all-to-all | bytes 4194304 | tf_op jit(solution)/shard_map/all_to_all | solution.py:25
  382.8 2.0 copy.55
  (48 shorter events, 5.9 us)
Async XLA Ops:
  7.2 190.8 %copy-start = (f32[512,64]{0,1:T(8,128)S(1)}, f32[512,64]{0,1:T(8,128)}, u32[]{:S(2)}) copy-start(f32[512,64]{0,1:T(8,128)} %param.6) | copy-start | bytes 393220
  7.2 129.2 %all-reduce.3.cloned.1.call-start = ((), (), s32[]{:S(2)}) async-start(), calls=%async_computation.1 | async-start | bytes 2097152 | tf_op jit(solution)/shard_map/psum | solution.py:20
  46.9 151.1 %all-reduce.5.cloned.1.call-start = ((), (), s32[]{:S(2)}) async-start(), calls=%async_computation.2 | async-start | bytes 2097152 | tf_op jit(solution)/shard_map/psum | solution.py:20
  319.3 65.4 %copy-start.1 = (f32[64,512]{1,0:T(8,128)}, f32[64,512]{1,0:T(8,128)S(1)}, u32[]{:S(2)}) copy-start(f32[64,512]{1,0:T(8,128)S(1)} %fusion.11) | copy-start | bytes 393220
Sparse Core Ops, SparseCore 0:
  47.0 89.3 all-reduce.2
  138.7 59.2 all-reduce.4
